TPU v7x, 256 devices: a whole 4x4x8 slice. The times are simulated.
256 devices in a mesh: head: 4 (over x), page: 64 (over y, z, core).
Axes of the slice: x: 4, y: 4, z: 8, core: 2. Of those that a mesh axis runs over, the one named last changes fastest.
Arguments:
- hidden: bfloat16 [12, 2048], P(None, 'page'), may hold values from -6 to 6
- q_weight: bfloat16 [2048, 3072], P('page', 'head'), may hold values from -0.125 to 0.125
- key_up: bfloat16 [16, 128, 512], P('head'), may hold values from -0.5 to 0.5
- value_up_weight: bfloat16 [16, 512, 128], P('head'), may hold values from -0.25 to 0.25
- out_weight: bfloat16 [2048, 2048], P('head', 'page'), may hold values from -0.125 to 0.125
- cache: bfloat16 [16, 512, 128, 576], P('head', 'page'), may hold values from -360 to 360
- page_table: int32 [16, 512], P('head', 'page'), may hold values from 0 to 511, each once within a row
- seq_pages: int32 [12], replicated, may hold values from 1 to 128, 512 in all
- keep_rows: int32 [16, 512, 64], P('head'), may hold values from 0 to 127, as said below
- fold_mass: bfloat16 [16, 512, 64], P('head'), may hold values from 0.5 to 4
- new_place: int32 [16, 512], P('head'), may hold values from 0 to 2047, as said below
- norm_gain: bfloat16 [2048], replicated, may hold values from 0.099609375 to 1.8984375
- router: bfloat16 [2048, 64], replicated, may hold values from -0.125 to 0.125
- routes: int32 [12, 6], replicated, may hold values from 0 to 63, all different within a row
- w_gate: bfloat16 [64, 2048, 1408], P('page', None, 'head'), may hold values from -0.125 to 0.125
- w_up: bfloat16 [64, 2048, 1408], P('page', None, 'head'), may hold values from -0.125 to 0.125
- w_down: bfloat16 [64, 1408, 2048], P('page', 'head'), may hold values from -0.15625 to 0.15625
Outputs:
- attn_out: bfloat16 [12, 2048], replicated
- moe_out: bfloat16 [12, 2048], replicated
- new_rows: bfloat16 [8192, 64, 576], P(('head', 'page'))
- new_mass: bfloat16 [8192, 64], P(('head', 'page'))
Inputs may be any that keep to these rules, and one draw needn't show every extreme that they name: `keep_rows`: the 64 entries of each head and page are distinct. `new_place`: for each group of heads h // 4 the places form a permutation of 0 to 2047. Among the blocks of one head group whose pages share g // 8, at most 1 have places with the same place // 32, and some reach 1.
All inputs are finite; a program needn't handle non-finite values.
Results may differ from a plain program's by a relative error of at most 0.035.
Values may be sent and summed in bfloat16 or wider, within the bound.
A program may use at most 128 MiB of HBM per device.

v0:
```python
import jax
import jax.numpy as jnp
from jax import lax
from jax.sharding import PartitionSpec as P

QK_NOPE = 128
QK_ROPE = 64
THETA = 50000.0
ROUTE_SCALE = 2.446
NORM_EPS = 1e-06


def joined_2(part, axis, combine):
    gathered = jax.tree.map(lambda a: lax.all_gather(a, axis), part)

    def take(source):
        return jax.tree.map(lambda a: lax.dynamic_index_in_dim(a, source, 0, False), gathered)

    return lax.fori_loop(
        1, lax.axis_size(axis), lambda source, state: combine(state, take(source)), take(0)
    )


def rotate_query(values, positions):
    half_dim = values.shape[-1] // 2
    freqs = THETA ** (-2.0 * jnp.arange(half_dim, dtype=jnp.float32) / values.shape[-1])
    angles = positions.astype(jnp.float32)[:, None] * freqs[None, :]
    cosine = jnp.cos(angles)[:, None, :]
    sine_v = jnp.sin(angles)[:, None, :]
    front = values[..., :half_dim]
    back = values[..., half_dim:]
    return jnp.concatenate(
        [front * cosine - back * sine_v, back * cosine + front * sine_v], axis=-1
    )


def pick_rows(one_page, row_ids):
    return one_page[row_ids]


def merge_parts(left_part, right_part):
    joined = jnp.maximum(left_part[0], right_part[0])
    left_factor = jnp.exp(left_part[0] - joined)
    right_factor = jnp.exp(right_part[0] - joined)
    return (
        joined,
        left_part[1] * left_factor + right_part[1] * right_factor,
        left_part[2] * left_factor[..., None] + right_part[2] * right_factor[..., None],
    )


def shards(
    hidden,
    q_weight,
    key_up,
    value_up_weight,
    out_weight,
    cache,
    page_table,
    seq_pages,
    keep_rows,
    fold_mass,
    new_place,
    norm_gain,
    router,
    routes,
    w_gate,
    w_up,
    w_down,
):
    heads_here = key_up.shape[0]
    pages_here = cache.shape[1]
    page_rows = cache.shape[2]
    latent_dim = cache.shape[3]
    kv_rank = key_up.shape[2]
    kept_count = keep_rows.shape[2]
    requests = hidden.shape[0]
    head_size = QK_NOPE + QK_ROPE
    groups = lax.axis_size("page")
    page_index = lax.axis_index("page")
    blocks = heads_here * pages_here
    sending_limit = (blocks + groups - 1) // groups
    first_page = page_index * pages_here
    partial_value = jnp.dot(hidden, q_weight, preferred_element_type=jnp.float32)
    queries = lax.psum(partial_value, "page").reshape(requests, heads_here, head_size)
    q_nope = queries[..., :QK_NOPE].astype(jnp.bfloat16)
    positions = seq_pages * page_rows - 1
    q_rope = rotate_query(queries[..., QK_NOPE:], positions).astype(jnp.bfloat16)
    q_latent = jnp.einsum(
        "rhn,hnk->rhk", q_nope, key_up, preferred_element_type=jnp.float32
    ).astype(jnp.bfloat16)
    q_full = jnp.concatenate([q_latent, q_rope], axis=-1)
    keep_here = lax.dynamic_slice_in_dim(keep_rows, first_page, pages_here, 1)
    mass_here = lax.dynamic_slice_in_dim(fold_mass, first_page, pages_here, 1)
    compact = jax.vmap(jax.vmap(pick_rows))(cache, keep_here)
    flat_rows = compact.reshape(heads_here, pages_here * kept_count, latent_dim)
    page_ends = jnp.cumsum(seq_pages)
    owner = jnp.sum((page_table[..., None] >= page_ends).astype(jnp.int32), axis=-1)
    row_owner = jnp.repeat(owner, kept_count, axis=1)
    in_request = row_owner[:, None, :] == jnp.arange(requests, dtype=jnp.int32)[None, :, None]
    scores = jnp.einsum(
        "rhk,hnk->hrn", q_full, flat_rows, preferred_element_type=jnp.float32
    ) * head_size ** (-0.5)
    row_max = jnp.max(jnp.where(in_request, scores, -1e30), axis=-1)
    row_mass = mass_here.reshape(heads_here, 1, pages_here * kept_count).astype(jnp.float32)
    weights = jnp.where(in_request, row_mass * jnp.exp(scores - row_max[..., None]), 0.0)
    totals = jnp.sum(weights, axis=-1)
    weighted = jnp.einsum(
        "hrn,hnk->hrk",
        weights.astype(jnp.bfloat16),
        flat_rows[..., :kv_rank],
        preferred_element_type=jnp.float32,
    )
    best, mass_sum, latent_sum = joined_2((row_max, totals, weighted), "page", merge_parts)
    latent_output = (latent_sum / mass_sum[..., None]).astype(jnp.bfloat16)
    head_result_rows = jnp.einsum(
        "usj,ujb->sub", latent_output, value_up_weight, preferred_element_type=jnp.float32
    ).astype(jnp.bfloat16)
    head_result_rows = head_result_rows.reshape(requests, heads_here * value_up_weight.shape[2])
    out_cols = jnp.dot(head_result_rows, out_weight, preferred_element_type=jnp.float32)
    col_width = out_cols.shape[1]
    padded = jnp.zeros((requests, col_width * groups), jnp.float32)
    padded = lax.dynamic_update_slice_in_dim(padded, out_cols, page_index * col_width, 1)
    attn_out = lax.psum(padded, ("head", "page")).astype(jnp.bfloat16)
    attn_wide = attn_out.astype(jnp.float32)
    mean_sq = jnp.mean(attn_wide * attn_wide, axis=-1, keepdims=True)
    normed = (attn_wide * lax.rsqrt(mean_sq + NORM_EPS) * norm_gain.astype(jnp.float32)).astype(
        jnp.bfloat16
    )
    logits = jnp.dot(normed, router, preferred_element_type=jnp.float32)
    picked = jax.nn.sigmoid(jnp.take_along_axis(logits, routes, axis=1))
    shares = ROUTE_SCALE * picked / jnp.sum(picked, axis=1, keepdims=True)
    expert_ids = jnp.arange(logits.shape[1], dtype=jnp.int32)
    combine = jnp.sum(
        jnp.where(routes[:, :, None] == expert_ids[None, None, :], shares[:, :, None], 0.0), axis=1
    )
    local_experts = w_gate.shape[0]
    combine_here = lax.dynamic_slice_in_dim(combine, page_index * local_experts, local_experts, 1)
    gate_part = jnp.einsum("rd,edf->erf", normed, w_gate, preferred_element_type=jnp.float32)
    up_part = jnp.einsum("rd,edf->erf", normed, w_up, preferred_element_type=jnp.float32)
    expert_hidden = (jax.nn.silu(gate_part) * up_part).astype(jnp.bfloat16)
    expert_outs = jnp.einsum(
        "erf,efd->erd", expert_hidden, w_down, preferred_element_type=jnp.float32
    )
    expert_terms = jnp.sum(combine_here.T[:, :, None] * expert_outs, axis=0)
    moe_out = lax.psum(expert_terms, ("head", "page")).astype(jnp.bfloat16)
    dest_all = new_place // blocks
    slot_all = new_place % blocks
    dest_here = lax.dynamic_slice_in_dim(dest_all, first_page, pages_here, 1).reshape(blocks)
    peer_ids = jnp.arange(groups, dtype=jnp.int32)
    dest_onehot = (dest_here[:, None] == peer_ids[None, :]).astype(jnp.int32)
    send_rank = jnp.sum(jnp.cumsum(dest_onehot, axis=0) * dest_onehot, axis=1) - 1
    send_col = dest_here * sending_limit + send_rank
    slot_ids = jnp.arange(groups * sending_limit, dtype=jnp.int32)
    chooser = (send_col[:, None] == slot_ids[None, :]).astype(jnp.bfloat16)

    def arrange(values):
        return (
            values.reshape(heads_here, groups, pages_here)
            .transpose(1, 0, 2)
            .reshape(groups, blocks)
        )

    to_here = arrange(dest_all) == page_index
    recv_rank = jnp.cumsum(to_here.astype(jnp.int32), axis=1) - 1
    recv_col = peer_ids[:, None] * sending_limit + recv_rank
    block_ids = jnp.arange(blocks, dtype=jnp.int32)
    by_slot = ((arrange(slot_all)[..., None] == block_ids) & to_here[..., None]).astype(
        jnp.bfloat16
    )
    by_col = (recv_col[..., None] == slot_ids).astype(jnp.bfloat16)
    unpack = jnp.einsum("sbq,sbc->qc", by_slot, by_col, preferred_element_type=jnp.float32).astype(
        jnp.bfloat16
    )
    owned = (slot_all.reshape(-1)[None, :] == block_ids[:, None]) & (
        dest_all.reshape(-1)[None, :] == page_index
    )
    new_mass = jnp.dot(
        owned.astype(jnp.bfloat16),
        fold_mass.reshape(-1, kept_count),
        preferred_element_type=jnp.float32,
    ).astype(jnp.bfloat16)
    payload = cache.reshape(blocks, page_rows * latent_dim)
    outgoing = jnp.einsum("bc,bx->cx", chooser, payload, preferred_element_type=jnp.float32).astype(
        jnp.bfloat16
    )
    arrived_rows = lax.all_to_all(
        outgoing.reshape(groups, sending_limit, page_rows, latent_dim),
        "page",
        split_axis=0,
        concat_axis=0,
        tiled=True,
    )
    placed = jnp.dot(
        unpack,
        arrived_rows.reshape(groups * sending_limit, page_rows * latent_dim),
        preferred_element_type=jnp.float32,
    ).astype(jnp.bfloat16)
    keep_new = jnp.dot(owned.astype(jnp.int32), keep_rows.reshape(-1, kept_count))
    new_rows = jax.vmap(pick_rows)(placed.reshape(blocks, page_rows, latent_dim), keep_new)
    return (attn_out, moe_out, new_rows, new_mass)


def solution(mesh):
    in_specs = (
        P(None, "page"),
        P("page", "head"),
        P("head", None, None),
        P("head", None, None),
        P("head", "page"),
        P("head", "page", None, None),
        P("head", "page"),
        P(),
        P("head", None, None),
        P("head", None, None),
        P("head", None),
        P(),
        P(),
        P(),
        P("page", None, "head"),
        P("page", None, "head"),
        P("page", "head", None),
    )
    out_specs = (P(), P(), P(("head", "page"), None, None), P(("head", "page"), None))
    return jax.shard_map(shards, mesh=mesh, in_specs=in_specs, out_specs=out_specs, check_vma=False)
```

profile of v0, /device:TPU:1, one launch (start us, length us, event | category | flops | bytes accessed | tf_op | source)
XLA Modules:
  0.0 994.9 jit_solution(4305672104055780673)
XLA Ops:
  7.3 1.1 constant_dynamic-slice_fusion.2
  8.6 7.8 copy.109
  16.6 249.7 %psum.21 = f32[12,4,192]{2,0,1:T(8,128)S(1)} all-reduce(f32[12,4,192]{2,0,1:T(8,128)S(1)} %copy.107), channel_id=1, replica_groups=mesh['head'=4,'page'=64] {'page'}, use_global_device_ids=true, to_apply=%region_2.3 | all-reduce | flops 9216 | bytes 73728 | tf_op jit(solution)/shard_map/psum | solution.py:85
  267.1 39.7 %gather_fusion = bf16[2048,576]{1,0:T(8,128)(2,1)} fusion(bf16[4,8,128,576]{3,2,1,0:T(8,128)(2,1)} %copy.109, s32[2048]{0:T(1024)S(1)} %reshape.256), kind=kCustom, calls=%fused_computation | custom fusion | bytes 4743168 | tf_op jit(solution)/shard_map/vmap(vmap())/gather | solution.py:38
  307.2 2.8 select_reduce_fusion
  310.0 1.1 fusion.3
  311.2 8.8 reshape.249
  320.5 8.7 convolution_convert_fusion
  329.2 15.5 %reshape.250 = bf16[64,1,128,576]{3,2,0,1:T(8,128)(2,1)} reshape(bf16[64,73728]{1,0:T(8,128)(2,1)} %convolution_convert_fusion) | data formatting | bytes 18874368 | tf_op jit(solution)/shard_map/reshape | solution.py:188
  344.7 13.9 %copy.123 = bf16[64,1,128,576]{2,3,1,0:T(8,128)(2,1)} copy(bf16[64,1,128,576]{3,2,0,1:T(8,128)(2,1)} %reshape.250) | data formatting | bytes 18874368 | tf_op jit(solution)/shard_map/reshape | solution.py:188
  358.6 10.9 %all-to-all-start = ((bf16[64,1,128,576]{2,3,1,0:T(8,128)(2,1)}), bf16[64,1,128,576]{2,3,1,0:T(8,128)(2,1)}, u32[]{:S(2)}, u32[]{:S(2)}) async-start(bf16[64,1,128,576]{2,3,1,0:T(8,128)(2,1)} %copy.123), calls=%async_computation | async-start | bytes 18874368 | tf_op jit(solution)/shard_map/all_to_all | solution.py:187
  371.6 259.4 %all-gather.4 = f32[64,4,12]{2,1,0:T(4,128)S(1)} all-gather(f32[1,4,12]{2,1,0:T(4,128)S(1)} %bitcast.156), channel_id=3, replica_groups=mesh['head'=4,'page'=64] {'page'}, dimensions={0}, use_global_device_ids=true | all-gather | bytes 12480 | tf_op jit(solution)/shard_map/all_gather | solution.py:14
  631.0 47.8 %all-gather.3 = f32[64,4,12]{2,1,0:T(4,128)S(1)} all-gather(f32[1,4,12]{2,1,0:T(4,128)S(1)} %bitcast.154), channel_id=2, replica_groups=mesh['head'=4,'page'=64] {'page'}, dimensions={0}, use_global_device_ids=true | all-gather | bytes 12480 | tf_op jit(solution)/shard_map/all_gather | solution.py:14
  680.5 66.4 %while.19 = (s32[]{:T(128)}, f32[4,12]{1,0:T(4,128)S(1)}, f32[4,12]{1,0:T(4,128)S(1)}, f32[4,12,512]{2,1,0:T(8,128)S(1)}, f32[64,4,12]{2,1,0:T(4,128)S(1)}, /*in...) while((s32[]{:T(128)}, f32[4,12]{1,0:T(4,128)S(1)}, ...), condition=%wide.region_6.7_spmd, body=%wide.region_5.6_spmd.sunk | while | flops 74021 | bytes 296983 | solution.py:19
  680.6 1.0 fusion.118
  681.6 1.0 fusion.118
  682.7 1.0 fusion.118
  683.7 1.0 fusion.118
  684.8 1.0 fusion.118
  685.8 1.0 fusion.118
  686.9 1.0 fusion.118
  689.0 1.0 fusion.118
  691.1 1.0 fusion.118
  693.2 1.0 fusion.118
  695.3 1.0 fusion.118
  697.4 1.0 fusion.118
  698.5 1.0 fusion.118
  699.5 1.0 fusion.118
  700.6 1.0 fusion.118
  701.6 1.0 fusion.118
  702.7 1.0 fusion.118
  703.8 1.0 fusion.118
  704.8 1.0 fusion.118
  705.9 1.0 fusion.118
  706.9 1.0 fusion.118
  709.0 1.0 fusion.118
  711.1 1.0 fusion.118
  713.2 1.0 fusion.118
  746.9 1.3 fusion.23
  748.8 75.9 %psum.22 = bf16[12,2048]{1,0:T(8,128)(2,1)S(1)} all-reduce(f32[12,2048]{1,0:T(8,128)S(1)} %dynamic_update_slice.3), channel_id=1, replica_groups=mesh['head'=4,'page'=64] {'head','page'}, use_global_device_ids=true, to_apply=%region_7.8 | all-reduce | flops 24576 | bytes 147456 | tf_op jit(solution)/shard_map/psum | solution.py:124
  825.1 1.7 gather_fusion.1
  827.9 2.5 convolution_multiply_fusion
  830.4 73.9 %psum.23 = bf16[12,2048]{1,0:T(8,128)(2,1)} all-reduce(f32[12,2048]{1,0:T(8,128)S(1)} %convolution_multiply_fusion), channel_id=1, replica_groups=mesh['head'=4,'page'=64] {'head','page'}, use_global_device_ids=true, to_apply=%region_11.12 | all-reduce | flops 24576 | bytes 147456 | tf_op jit(solution)/shard_map/psum | solution.py:146
  904.3 14.1 %copy.124 = bf16[64,1,128,576]{3,2,0,1:T(8,128)(2,1)} copy(bf16[64,1,128,576]{2,3,1,0:T(8,128)(2,1)} %all-to-all-done) | data formatting | bytes 18874368 | tf_op jit(solution)/shard_map/all_to_all | solution.py:187
  918.4 15.3 %reshape.251 = bf16[64,73728]{1,0:T(8,128)(2,1)} reshape(bf16[64,1,128,576]{3,2,0,1:T(8,128)(2,1)} %copy.124) | data formatting | bytes 18874368 | tf_op jit(solution)/shard_map/reshape | solution.py:196
  933.6 8.0 convolution_convert_fusion.1
  941.7 8.8 reshape.252
  950.5 37.5 %gather_fusion.2 = bf16[2048,576]{1,0:T(8,128)(2,1)} fusion(bf16[32,128,576]{2,1,0:T(8,128)(2,1)} %reshape.252, s32[2048]{0:T(1024)S(1)} %reshape.268), kind=kCustom, calls=%fused_computation.2 | custom fusion | bytes 4734976 | tf_op jit(solution)/shard_map/vmap()/gather | solution.py:38
  (208 shorter events, 48.6 us)
Async XLA Ops:
  7.2 820.7 %copy-start = (bf16[1,352,2048]{2,1,0:T(8,128)(2,1)S(1)}, bf16[1,352,2048]{2,1,0:T(8,128)(2,1)}, u32[]{:S(2)}) copy-start(bf16[1,352,2048]{2,1,0:T(8,128)(2,1)} %param.35) | copy-start | bytes 4325380
  7.2 672.4 %all-gather.7.cloned.1.call-start = ((), (), s32[]{:S(2)}) async-start(), calls=%async_computation.1 | async-start | bytes 8519680 | tf_op jit(solution)/shard_map/all_gather | solution.py:14
  8.5 7.8 copy-start.8
  8.5 7.8 copy-start.11
  8.5 257.7 %copy-start.15 = (s32[12]{0:T(128)S(1)}, s32[12]{0:T(128)}, u32[]{:S(2)}) copy-start(s32[12]{0:T(128)} %param.26) | copy-start | bytes 148
  8.5 257.9 %copy-start.13 = (s32[4,8]{1,0:T(4,128)S(1)}, s32[4,8]{1,0:T(4,128)}, u32[]{:S(2)}) copy-start(s32[4,8]{1,0:T(4,128)} %param.25) | copy-start | bytes 388
  8.5 258.3 %copy-start.6 = (bf16[4,512,64]{1,2,0:T(8,128)(2,1)S(1)}, bf16[4,512,64]{1,2,0:T(8,128)(2,1)}, u32[]{:S(2)}) copy-start(bf16[4,512,64]{1,2,0:T(8,128)(2,1)} %param.28) | copy-start | bytes 786436
  267.1 39.8 %copy-start.5 = (bf16[4,128,512]{2,1,0:T(8,128)(2,1)S(1)}, bf16[4,128,512]{2,1,0:T(8,128)(2,1)}, u32[]{:S(2)}) copy-start(bf16[4,128,512]{2,1,0:T(8,128)(2,1)} %param.21) | copy-start | bytes 1572868
  306.8 3.2 copy-start.1
  311.2 8.8 copy-start.7
  358.6 10.9 %copy-start.12 = (bf16[2048]{0:T(1024)(128)(2,1)S(1)}, bf16[2048]{0:T(1024)(128)(2,1)}, u32[]{:S(2)}) copy-start(bf16[2048]{0:T(1024)(128)(2,1)} %param.30) | copy-start | bytes 12292
  358.6 10.9 %copy-start.9 = (s32[12,6]{0,1:T(8,128)S(1)}, s32[12,6]{0,1:T(8,128)}, u32[]{:S(2)}) copy-start(s32[12,6]{0,1:T(8,128)} %param.32) | copy-start | bytes 868
  358.6 12.2 %copy-start.4 = (s32[4,512,64]{1,2,0:T(8,128)S(1)}, s32[4,512,64]{1,2,0:T(8,128)}, u32[]{:S(2)}) copy-start(s32[4,512,64]{1,2,0:T(8,128)} %param.27) | copy-start | bytes 1572868
  358.6 545.7 %all-to-all-start = ((bf16[64,1,128,576]{2,3,1,0:T(8,128)(2,1)}), bf16[64,1,128,576]{2,3,1,0:T(8,128)(2,1)}, u32[]{:S(2)}, u32[]{:S(2)}) async-start(bf16[64,1,128,576]{2,3,1,0:T(8,128)(2,1)} %copy.123), calls=%async_computation | async-start | bytes 18874368 | tf_op jit(solution)/shard_map/all_to_all | solution.py:187
  370.8 377.4 %copy-start.10 = (bf16[512,32]{0,1:T(8,128)(2,1)S(1)}, bf16[512,32]{0,1:T(8,128)(2,1)}, u32[]{:S(2)}) copy-start(bf16[512,32]{0,1:T(8,128)(2,1)} %param.23) | copy-start | bytes 98308
  371.4 453.5 %copy-start.14 = (bf16[2048,64]{0,1:T(8,128)(2,1)S(1)}, bf16[2048,64]{0,1:T(8,128)(2,1)}, u32[]{:S(2)}) copy-start(bf16[2048,64]{0,1:T(8,128)(2,1)} %param.31) | copy-start | bytes 786436
  824.7 3.2 copy-start.3
  825.1 2.3 copy-start.2
Sparse Core Ops, SparseCore 0:
  311.3 121.7 all-gather.6
where the time goes:
time: 999 us; the launch traced here: 995 us
  blocking collectives  707 us (71%)
  local copies, waits for them, and re-layouts  168 us (17%)
  other arithmetic  66.3 us (7%)
  matrix products  26.8 us (3%)
  between operations  14.4 us (1%)
  starting transfers between devices  10.9 us (1%)
    all_gather x2, blocking collectives, joined_2(): gathered = jax.tree.map(lambda a: lax.all_gather(a, axis), part)  307 us
    psum x1, blocking collectives, shards(): lax.psum(partial_value, 'page').reshape(requests, heads_here, head_size)  250 us
    gather x4, local copies, waits for them, and re-layouts, pick_rows(): return one_page[row_ids]  77.4 us
    psum x1, blocking collectives, shards(): attn_out = lax.psum(padded, ('head', 'page')).astype(jnp.bfloat16)  75.9 us
    psum x1, blocking collectives, shards(): moe_out = lax.psum(expert_terms, ('head', 'page')).astype(jnp.bfloat16)  73.9 us
    add x63, other arithmetic, merge_parts(): left_part[2] * left_factor[..., None]  62.9 us
    reshape x2, local copies, waits for them, and re-layouts, shards(): outgoing.reshape(groups, sending_limit, page_rows, latent_dim)  29.4 us
  transfers between devices with their start and end apart: 2, of which 0 were waited for; matrix products, arithmetic and copies ran while one was open for 12% of the time, Pallas kernels for 0%

commit v1 on v0

--- a/solution.py
+++ b/solution.py
@@ -143,7 +143,7 @@
         "erf,efd->erd", expert_hidden, w_down, preferred_element_type=jnp.float32
     )
     expert_terms = jnp.sum(combine_here.T[:, :, None] * expert_outs, axis=0)
-    moe_out = lax.psum(expert_terms, ("head", "page")).astype(jnp.bfloat16)
+    moe_out = lax.psum(lax.psum(expert_terms, "head"), "page").astype(jnp.bfloat16)
     dest_all = new_place // blocks
     slot_all = new_place % blocks
     dest_here = lax.dynamic_slice_in_dim(dest_all, first_page, pages_here, 1).reshape(blocks)

time: 999 us -> 1220 us (1.22)
  blocking collectives: 707 us -> 880 us
  waiting for transfers between devices: 0.02 us -> 39.8 us
    psum x1, blocking collectives: 73.9 us -> 246 us  [shards(): lax.psum(lax.psum(expert_terms, 'head'), 'page').astype(jnp.bfloat16)]
    psum x0 -> x1, waiting for transfers between devices: none -> 39.8 us  [shards(): lax.psum(expert_terms, 'head')]
  transfers between devices with their start and end apart: 2 -> 3, of which waited for: 0 -> 1; matrix products, arithmetic and copies ran while one was open for 12% -> 10% of each run, Pallas kernels for 0% -> 0%
where the time goes in v1:
time: 1220 us; the launch traced here: 1210 us
  blocking collectives  880 us (72%)
  local copies, waits for them, and re-layouts  168 us (14%)
  other arithmetic  66.3 us (5%)
  waiting for transfers between devices  39.8 us (3%)
  matrix products  27.5 us (2%)
  between operations  14.4 us (1%)
    all_gather x2, blocking collectives, joined_2(): gathered = jax.tree.map(lambda a: lax.all_gather(a, axis), part)  308 us
    psum x1, blocking collectives, shards(): lax.psum(partial_value, 'page').reshape(requests, heads_here, head_size)  250 us
    psum x1, blocking collectives, shards(): lax.psum(lax.psum(expert_terms, 'head'), 'page').astype(jnp.bfloat16)  246 us
    gather x4, local copies, waits for them, and re-layouts, pick_rows(): return one_page[row_ids]  77.4 us
    psum x1, blocking collectives, shards(): attn_out = lax.psum(padded, ('head', 'page')).astype(jnp.bfloat16)  75.9 us
    add x63, other arithmetic, merge_parts(): left_part[2] * left_factor[..., None]  63 us
    psum x1, waiting for transfers between devices, shards(): lax.psum(expert_terms, 'head')  39.8 us
    reshape x2, local copies, waits for them, and re-layouts, shards(): outgoing.reshape(groups, sending_limit, page_rows, latent_dim)  29.4 us
  transfers between devices with their start and end apart: 3, of which 1 were waited for; matrix products, arithmetic and copies ran while one was open for 10% of the time, Pallas kernels for 0%

profile of v1, /device:TPU:1, one launch (start us, length us, event | category | flops | bytes accessed | tf_op | source)
XLA Modules:
  0.0 1208.3 jit_solution(18075648314767954642)
XLA Ops:
  7.3 1.1 constant_dynamic-slice_fusion.2
  8.6 7.8 copy.109
  16.6 249.7 %psum.28 = f32[12,4,192]{2,0,1:T(8,128)S(1)} all-reduce(f32[12,4,192]{2,0,1:T(8,128)S(1)} %copy.107), channel_id=1, replica_groups=mesh['head'=4,'page'=64] {'page'}, use_global_device_ids=true, to_apply=%region_2.3 | all-reduce | flops 9216 | bytes 73728 | tf_op jit(solution)/shard_map/psum | solution.py:85
  267.1 39.7 %gather_fusion = bf16[2048,576]{1,0:T(8,128)(2,1)} fusion(bf16[4,8,128,576]{3,2,1,0:T(8,128)(2,1)} %copy.109, s32[2048]{0:T(1024)S(1)} %reshape.256), kind=kCustom, calls=%fused_computation | custom fusion | bytes 4743168 | tf_op jit(solution)/shard_map/vmap(vmap())/gather | solution.py:38
  307.2 2.8 select_reduce_fusion
  310.0 1.1 fusion.3
  311.2 8.8 reshape.249
  320.5 8.7 convolution_convert_fusion
  329.2 15.5 %reshape.250 = bf16[64,1,128,576]{3,2,0,1:T(8,128)(2,1)} reshape(bf16[64,73728]{1,0:T(8,128)(2,1)} %convolution_convert_fusion) | data formatting | bytes 18874368 | tf_op jit(solution)/shard_map/reshape | solution.py:188
  344.6 13.9 %copy.123 = bf16[64,1,128,576]{2,3,1,0:T(8,128)(2,1)} copy(bf16[64,1,128,576]{3,2,0,1:T(8,128)(2,1)} %reshape.250) | data formatting | bytes 18874368 | tf_op jit(solution)/shard_map/reshape | solution.py:188
  358.6 10.9 all-to-all-start
  370.7 260.3 %all-gather.4 = f32[64,4,12]{2,1,0:T(4,128)S(1)} all-gather(f32[1,4,12]{2,1,0:T(4,128)S(1)} %bitcast.156), channel_id=3, replica_groups=mesh['head'=4,'page'=64] {'page'}, dimensions={0}, use_global_device_ids=true | all-gather | bytes 12480 | tf_op jit(solution)/shard_map/all_gather | solution.py:14
  631.0 47.8 %all-gather.3 = f32[64,4,12]{2,1,0:T(4,128)S(1)} all-gather(f32[1,4,12]{2,1,0:T(4,128)S(1)} %bitcast.154), channel_id=2, replica_groups=mesh['head'=4,'page'=64] {'page'}, dimensions={0}, use_global_device_ids=true | all-gather | bytes 12480 | tf_op jit(solution)/shard_map/all_gather | solution.py:14
  681.0 66.4 %while.19 = (s32[]{:T(128)}, f32[4,12]{1,0:T(4,128)S(1)}, f32[4,12]{1,0:T(4,128)S(1)}, f32[4,12,512]{2,1,0:T(8,128)S(1)}, f32[64,4,12]{2,1,0:T(4,128)S(1)}, /*in...) while((s32[]{:T(128)}, f32[4,12]{1,0:T(4,128)S(1)}, ...), condition=%wide.region_6.7_spmd, body=%wide.region_5.6_spmd.sunk | while | flops 74021 | bytes 296983 | solution.py:19
  681.0 1.0 fusion.118
  683.2 1.0 fusion.118
  684.2 1.0 fusion.118
  685.3 1.0 fusion.118
  688.4 1.0 fusion.118
  689.5 1.0 fusion.118
  690.5 1.0 fusion.118
  693.7 1.0 fusion.118
  694.7 1.0 fusion.118
  695.8 1.0 fusion.118
  697.9 1.0 fusion.118
  699.0 1.0 fusion.118
  700.0 1.0 fusion.118
  701.1 1.0 fusion.118
  703.2 1.0 fusion.118
  704.2 1.0 fusion.118
  705.3 1.0 fusion.118
  708.4 1.0 fusion.118
  709.5 1.0 fusion.118
  710.5 1.0 fusion.118
  713.7 1.0 fusion.118
  714.8 1.0 fusion.118
  715.8 1.0 fusion.118
  747.4 1.3 fusion.23
  749.2 75.9 %psum.29 = bf16[12,2048]{1,0:T(8,128)(2,1)S(1)} all-reduce(f32[12,2048]{1,0:T(8,128)S(1)} %dynamic_update_slice.3), channel_id=1, replica_groups=mesh['head'=4,'page'=64] {'head','page'}, use_global_device_ids=true, to_apply=%region_7.8 | all-reduce | flops 24576 | bytes 147456 | tf_op jit(solution)/shard_map/psum | solution.py:124
  825.5 1.7 gather_fusion.1
  828.3 3.2 convolution_multiply_fusion
  832.0 39.8 %all-reduce.2.cloned.1.call-done = f32[12,2048]{1,0:T(8,128)} async-done(((f32[12,2048]{1,0:T(8,128)}), f32[12,2048]{1,0:T(8,128)}) %all-reduce.2.cloned.1.call-update) | async-done | bytes 98320 | tf_op jit(solution)/shard_map/psum | solution.py:146
  871.8 246.0 %psum.31 = bf16[12,2048]{1,0:T(8,128)(2,1)} all-reduce(f32[12,2048]{1,0:T(8,128)} %all-reduce.2.cloned.1.call-done), channel_id=1, replica_groups=mesh['head'=4,'page'=64] {'page'}, use_global_device_ids=true, to_apply=%region_12.13 | all-reduce | flops 24576 | bytes 147456 | tf_op jit(solution)/shard_map/psum | solution.py:146
  1117.8 14.1 %copy.124 = bf16[64,1,128,576]{3,2,0,1:T(8,128)(2,1)} copy(bf16[64,1,128,576]{2,3,1,0:T(8,128)(2,1)} %all-to-all-done) | data formatting | bytes 18874368 | tf_op jit(solution)/shard_map/all_to_all | solution.py:187
  1131.8 15.3 %reshape.251 = bf16[64,73728]{1,0:T(8,128)(2,1)} reshape(bf16[64,1,128,576]{3,2,0,1:T(8,128)(2,1)} %copy.124) | data formatting | bytes 18874368 | tf_op jit(solution)/shard_map/reshape | solution.py:196
  1147.1 8.0 convolution_convert_fusion.1
  1155.2 8.8 reshape.252
  1164.0 37.5 %gather_fusion.2 = bf16[2048,576]{1,0:T(8,128)(2,1)} fusion(bf16[32,128,576]{2,1,0:T(8,128)(2,1)} %reshape.252, s32[2048]{0:T(1024)S(1)} %reshape.268), kind=kCustom, calls=%fused_computation.2 | custom fusion | bytes 4734976 | tf_op jit(solution)/shard_map/vmap()/gather | solution.py:38
  (211 shorter events, 49.6 us)
Async XLA Ops:
  7.2 821.2 %copy-start = (bf16[1,352,2048]{2,1,0:T(8,128)(2,1)S(1)}, bf16[1,352,2048]{2,1,0:T(8,128)(2,1)}, u32[]{:S(2)}) copy-start(bf16[1,352,2048]{2,1,0:T(8,128)(2,1)} %param.35) | copy-start | bytes 4325380
  7.2 672.9 %all-gather.7.cloned.1.call-start = ((), (), s32[]{:S(2)}) async-start(), calls=%async_computation.2 | async-start | bytes 8519680 | tf_op jit(solution)/shard_map/all_gather | solution.py:14
  8.5 7.8 copy-start.8
  8.5 7.8 copy-start.11
  8.5 257.7 %copy-start.15 = (s32[12]{0:T(128)S(1)}, s32[12]{0:T(128)}, u32[]{:S(2)}) copy-start(s32[12]{0:T(128)} %param.26) | copy-start | bytes 148
  8.5 257.9 %copy-start.13 = (s32[4,8]{1,0:T(4,128)S(1)}, s32[4,8]{1,0:T(4,128)}, u32[]{:S(2)}) copy-start(s32[4,8]{1,0:T(4,128)} %param.25) | copy-start | bytes 388
  8.5 258.3 %copy-start.6 = (bf16[4,512,64]{1,2,0:T(8,128)(2,1)S(1)}, bf16[4,512,64]{1,2,0:T(8,128)(2,1)}, u32[]{:S(2)}) copy-start(bf16[4,512,64]{1,2,0:T(8,128)(2,1)} %param.28) | copy-start | bytes 786436
  267.1 39.8 %copy-start.5 = (bf16[4,128,512]{2,1,0:T(8,128)(2,1)S(1)}, bf16[4,128,512]{2,1,0:T(8,128)(2,1)}, u32[]{:S(2)}) copy-start(bf16[4,128,512]{2,1,0:T(8,128)(2,1)} %param.21) | copy-start | bytes 1572868
  306.8 3.2 copy-start.1
  311.2 8.8 copy-start.7
  358.6 10.9 copy-start.12
  358.6 11.0 copy-start.9
  358.6 11.8 copy-start.4
  358.6 759.2 %all-to-all-start = ((bf16[64,1,128,576]{2,3,1,0:T(8,128)(2,1)}), bf16[64,1,128,576]{2,3,1,0:T(8,128)(2,1)}, u32[]{:S(2)}, u32[]{:S(2)}) async-start(bf16[64,1,128,576]{2,3,1,0:T(8,128)(2,1)} %copy.123), calls=%async_computation | async-start | bytes 18874368 | tf_op jit(solution)/shard_map/all_to_all | solution.py:187
  369.5 502.3 %all-reduce.2.cloned.1.call-start = ((), (), s32[]{:S(2)}) async-start(), calls=%async_computation.1 | async-start | bytes 262144 | tf_op jit(solution)/shard_map/psum | solution.py:146
  370.5 378.3 %copy-start.10 = (bf16[512,32]{0,1:T(8,128)(2,1)S(1)}, bf16[512,32]{0,1:T(8,128)(2,1)}, u32[]{:S(2)}) copy-start(bf16[512,32]{0,1:T(8,128)(2,1)} %param.23) | copy-start | bytes 98308
  370.5 454.8 %copy-start.14 = (bf16[2048,64]{0,1:T(8,128)(2,1)S(1)}, bf16[2048,64]{0,1:T(8,128)(2,1)}, u32[]{:S(2)}) copy-start(bf16[2048,64]{0,1:T(8,128)(2,1)} %param.31) | copy-start | bytes 786436
  825.1 3.2 copy-start.3
  825.5 2.3 copy-start.2
Sparse Core Ops, SparseCore 0:
  311.3 121.7 all-gather.6
  831.6 40.0 all-reduce.1
